TPU v7x, 256 devices: a whole 4x4x8 slice. The times are simulated.
256 devices in a mesh: row: 16 (over z, core), col: 16 (over x, y).
Axes of the slice: x: 4, y: 4, z: 8, core: 2. Of those that a mesh axis runs over, the one named last changes fastest.
Arguments:
- tiles: float32 [16, 16, 16, 128, 128], P('row', 'col'), may hold values from -1 to 1
- tile_rows: int32 [16, 16, 16], P('row', 'col'), may hold values from 0 to 63, as said below
- tile_cols: int32 [16, 16, 16], P('row', 'col'), may hold values from 0 to 63
- tile_counts: int32 [16, 16], P('row', 'col'), may hold values from 2 to 16, as said below
- objective: float32 [131072], P('col'), may hold values from -6 to 6
- upper: float32 [131072], P('col'), may hold values from 0.2 to 2
- bound_codes: int32 [131072], P('col'), may hold values from 0 to 2
- rhs: float32 [131072], P('row'), may hold values from -6 to 6
- row_codes: int32 [131072], P('row'), may hold values from 0 to 1
Outputs:
- primal: float32 [131072], P('col')
- dual: float32 [131072], P('row')
Inputs may be any that keep to these rules, and one draw needn't show every extreme that they name: `tile_rows`: one device's live slots hold distinct (tile row, tile column) pairs. `tile_counts`: slots at or past a device's count are not part of K; some device has all 16 slots live.
All inputs are finite; a program needn't handle non-finite values. Where the computation divides by a largest or mean magnitude, that divisor is 1e-20 or more.
Results may differ from a plain program's by a relative error of at most 0.00018.
Values sent between devices are 32-bit elements; how exact they have to be, the bound alone decides.
A program may use at most 64 MiB of HBM per device.

v0:
```python
import jax
import jax.numpy as jnp
from jax import lax
from jax.sharding import PartitionSpec as P

TILE_BLOCK = 16
TILE_ROWS = 64
TILE_COLS = 64
OUTER = 2
INNER = 4


def project_primal(values, bound_codes, upper):
    values = jnp.where(bound_codes >= 1, jnp.maximum(values, 0.0), values)
    return jnp.where(bound_codes == 2, jnp.minimum(values, upper), values)


def project_dual(values, row_codes):
    return jnp.where(row_codes == 1, jnp.maximum(values, 0.0), values)


def step_update(step_size, weight, inter_term, primal_sq, dual_sq, counter):
    shrink = 1.0 - (counter + 1) ** (-0.3)
    growth = 1.0 + (counter + 1) ** (-0.6)
    numer = shrink * (weight * primal_sq + dual_sq / weight + 1e-06)
    return numer / jnp.maximum(2.0 * jnp.abs(inter_term), numer / (growth * step_size))


def tile_products(tile_data, row_slots, col_slots, live_count, vector, direction):
    highest = lax.Precision.HIGHEST
    width = tile_data.shape[-1]
    groups = (live_count + TILE_BLOCK - 1) // TILE_BLOCK
    if direction == "forward":
        shaped = vector.reshape(TILE_COLS, width)
        out_rows = TILE_ROWS
    else:
        shaped = vector.reshape(TILE_ROWS, width)
        out_rows = TILE_COLS

    def visit(group, total):
        first_slot = group * TILE_BLOCK
        alive = (first_slot + jnp.arange(TILE_BLOCK, dtype=jnp.int32) < live_count).astype(
            jnp.float32
        )
        row_hot = (row_slots[:, None] == jnp.arange(TILE_ROWS, dtype=jnp.int32)[None, :]).astype(
            jnp.float32
        )
        col_hot = (col_slots[:, None] == jnp.arange(TILE_COLS, dtype=jnp.int32)[None, :]).astype(
            jnp.float32
        )
        if direction == "forward":
            pieces = jnp.dot(col_hot, shaped, precision=highest)
            images = jnp.einsum("tij,tj->ti", tile_data, pieces, precision=highest)
            return total + jnp.einsum(
                "tk,ti->ki", row_hot * alive[:, None], images, precision=highest
            )
        else:
            pieces = jnp.dot(row_hot, shaped, precision=highest)
            images = jnp.einsum("tij,ti->tj", tile_data, pieces, precision=highest)
            return total + jnp.einsum(
                "tk,tj->kj", col_hot * alive[:, None], images, precision=highest
            )

    total = lax.fori_loop(0, groups, visit, jnp.zeros((out_rows, width), jnp.float32))
    return total.reshape(-1)


def per_device(
    tiles, tile_rows, tile_cols, tile_counts, objective, upper, bound_codes, rhs, row_codes
):
    tile_data = tiles[0, 0]
    row_slots = tile_rows[0, 0]
    col_slots = tile_cols[0, 0]
    live_count = tile_counts[0, 0]
    row_place = lax.axis_index("row")
    col_place = lax.axis_index("col")
    primal_mask = (row_place == 0).astype(jnp.float32)
    dual_mask = (col_place == 0).astype(jnp.float32)

    def forward(vector):
        partial_rows = tile_products(tile_data, row_slots, col_slots, live_count, vector, "forward")
        return lax.psum(partial_rows, "col")

    def backward(vector):
        partial_cols = tile_products(
            tile_data, row_slots, col_slots, live_count, vector, "backward"
        )
        return lax.psum(partial_cols, "row")

    def pair_sums(primal_term, dual_term):
        return lax.psum((primal_term * primal_mask, dual_term * dual_mask), ("row", "col"))

    alive_slots = (jnp.arange(tile_data.shape[0], dtype=jnp.int32) < live_count).astype(jnp.float32)
    local_largest = jnp.max(jnp.abs(tile_data) * alive_slots[:, None, None])
    largest = lax.pmax(local_largest, ("row", "col"))
    step_size = 0.05 / (largest + 1e-06)
    object_sq, rhs_sq = pair_sums(jnp.sum(objective * objective), jnp.sum(rhs * rhs))
    weight = jnp.sqrt((object_sq + 1e-06) / (rhs_sq + 1e-06))
    primal = jnp.zeros_like(objective)
    dual_piece = jnp.zeros_like(rhs)
    row_image = jnp.zeros_like(rhs)
    col_image = jnp.zeros_like(objective)
    counter = 0
    for cycle_index in range(OUTER):
        start_primal = primal
        start_dual = dual_piece
        primal_total = jnp.zeros_like(objective)
        dual_total = jnp.zeros_like(rhs)
        weight_total = jnp.zeros((), jnp.float32)
        for step_index in range(INNER):
            counter += 1
            next_primal = project_primal(
                primal - step_size / weight * (objective - col_image), bound_codes, upper
            )
            next_row = forward(next_primal)
            next_dual = project_dual(
                dual_piece + step_size * weight * (rhs - (2.0 * next_row - row_image)), row_codes
            )
            next_col = backward(next_dual)
            primal_move = next_primal - primal
            dual_move = next_dual - dual_piece
            inter_term, primal_sq, dual_sq = lax.psum(
                (
                    jnp.sum(primal_move * (next_col - col_image)) * primal_mask,
                    jnp.sum(primal_move * primal_move) * primal_mask,
                    jnp.sum(dual_move * dual_move) * dual_mask,
                ),
                ("row", "col"),
            )
            primal_total = primal_total + step_size * next_primal
            dual_total = dual_total + step_size * next_dual
            weight_total = weight_total + step_size
            step_size = step_update(step_size, weight, inter_term, primal_sq, dual_sq, counter)
            primal, dual_piece, row_image, col_image = (next_primal, next_dual, next_row, next_col)
        primal = primal_total / weight_total
        dual_piece = dual_total / weight_total
        primal_shift = primal - start_primal
        dual_shift = dual_piece - start_dual
        primal_drift, dual_drift = pair_sums(
            jnp.sum(primal_shift * primal_shift), jnp.sum(dual_shift * dual_shift)
        )
        weight = jnp.sqrt(weight * jnp.sqrt(dual_drift + 1e-06) / jnp.sqrt(primal_drift + 1e-06))
        if cycle_index + 1 < OUTER:
            row_image = forward(primal)
            col_image = backward(dual_piece)
    return (primal, dual_piece)


def solution(mesh):
    placed = (
        P("row", "col", None, None, None),
        P("row", "col", None),
        P("row", "col", None),
        P("row", "col"),
        P("col"),
        P("col"),
        P("col"),
        P("row"),
        P("row"),
    )
    return jax.shard_map(
        per_device, mesh=mesh, in_specs=placed, out_specs=(P("col"), P("row")), check_vma=False
    )
```

profile of v0, /device:TPU:32, one launch (start us, length us, event | category | flops | bytes accessed | tf_op | source)
XLA Modules:
  0.0 1723.5 jit_solution(5136370811758483441)
XLA Ops:
  10.5 79.8 %all-reduce.7 = (f32[]{:T(128)}, f32[]{:T(128)}) all-reduce(f32[]{:T(128)S(6)} %mul.700, f32[]{:T(128)S(6)} %mul.702), channel_id=1, replica_groups=mesh['row'=16,'col'=16] {'row','col'}, use_global_device_ids=true, to_apply=%region_1.0 | all-reduce | flops 2 | bytes 16 | tf_op jit(solution)/shard_map/psum | solution.py:91
  91.7 2.2 fusion.120
  93.9 73.6 %pmax.7 = f32[]{:T(128)} all-reduce(f32[]{:T(128)} %fusion.120), channel_id=1, replica_groups=mesh['row'=16,'col'=16] {'row','col'}, use_global_device_ids=true, to_apply=%region_5.0 | all-reduce | flops 1 | bytes 8 | tf_op jit(solution)/shard_map/pmax | solution.py:95
  169.1 1.7 fusion.117
  172.5 70.9 %psum.297 = f32[8192]{0:T(1024)S(1)} all-reduce(f32[8192]{0:T(1024)S(1)} %bitcast.318), channel_id=1, replica_groups=mesh['row'=16,'col'=16] {'col'}, use_global_device_ids=true, to_apply=%region_10.11 | all-reduce | flops 8192 | bytes 65536 | tf_op jit(solution)/shard_map/psum | solution.py:82
  246.2 42.2 %psum.299 = f32[8192]{0:T(1024)S(1)} all-reduce(f32[8192]{0:T(1024)S(1)} %bitcast.319), channel_id=1, replica_groups=mesh['row'=16,'col'=16] {'row'}, use_global_device_ids=true, to_apply=%region_15.16 | all-reduce | flops 8192 | bytes 65536 | tf_op jit(solution)/shard_map/psum | solution.py:88
  291.1 74.6 %all-reduce.6 = (f32[]{:T(128)}, f32[]{:T(128)}, f32[]{:T(128)}) all-reduce(f32[]{:T(128)S(6)} %mul.708, f32[]{:T(128)S(6)} %mul.715, f32[]{:T(128)S(6)} %mul.717), channel_id=1, replica_groups=mesh['row'=16,'col'=16] {'row','col'}, use_global_device_ids=true, to_apply=%region_7.8 | all-reduce | flops 3 | bytes 24 | tf_op jit(solution)/shard_map/psum | solution.py:122
  370.6 71.0 %psum.302 = f32[8192]{0:T(1024)S(1)} all-reduce(f32[8192]{0:T(1024)S(1)} %bitcast.320), channel_id=1, replica_groups=mesh['row'=16,'col'=16] {'col'}, use_global_device_ids=true, to_apply=%region_22.23 | all-reduce | flops 8192 | bytes 65536 | tf_op jit(solution)/shard_map/psum | solution.py:82
  444.4 42.2 %psum.304 = f32[8192]{0:T(1024)S(1)} all-reduce(f32[8192]{0:T(1024)S(1)} %bitcast.321), channel_id=1, replica_groups=mesh['row'=16,'col'=16] {'row'}, use_global_device_ids=true, to_apply=%region_27.28 | all-reduce | flops 8192 | bytes 65536 | tf_op jit(solution)/shard_map/psum | solution.py:88
  489.3 74.6 %all-reduce.5 = (f32[]{:T(128)}, f32[]{:T(128)}, f32[]{:T(128)}) all-reduce(f32[]{:T(128)S(6)} %mul.722, f32[]{:T(128)S(6)} %mul.729, f32[]{:T(128)S(6)} %mul.731), channel_id=1, replica_groups=mesh['row'=16,'col'=16] {'row','col'}, use_global_device_ids=true, to_apply=%region_19.20 | all-reduce | flops 3 | bytes 24 | tf_op jit(solution)/shard_map/psum | solution.py:122
  566.1 1.7 fusion.109
  568.8 71.0 %psum.307 = f32[8192]{0:T(1024)S(1)} all-reduce(f32[8192]{0:T(1024)S(1)} %bitcast.322), channel_id=1, replica_groups=mesh['row'=16,'col'=16] {'col'}, use_global_device_ids=true, to_apply=%region_34.35 | all-reduce | flops 8192 | bytes 65536 | tf_op jit(solution)/shard_map/psum | solution.py:82
  642.6 42.2 %psum.309 = f32[8192]{0:T(1024)S(1)} all-reduce(f32[8192]{0:T(1024)S(1)} %bitcast.323), channel_id=1, replica_groups=mesh['row'=16,'col'=16] {'row'}, use_global_device_ids=true, to_apply=%region_39.40 | all-reduce | flops 8192 | bytes 65536 | tf_op jit(solution)/shard_map/psum | solution.py:88
  687.5 74.6 %all-reduce.4 = (f32[]{:T(128)}, f32[]{:T(128)}, f32[]{:T(128)}) all-reduce(f32[]{:T(128)S(6)} %mul.736, f32[]{:T(128)S(6)} %mul.743, f32[]{:T(128)S(6)} %mul.745), channel_id=1, replica_groups=mesh['row'=16,'col'=16] {'row','col'}, use_global_device_ids=true, to_apply=%region_31.32 | all-reduce | flops 3 | bytes 24 | tf_op jit(solution)/shard_map/psum | solution.py:122
  765.0 1.7 fusion.105
  767.7 71.0 %psum.312 = f32[8192]{0:T(1024)S(1)} all-reduce(f32[8192]{0:T(1024)S(1)} %bitcast.324), channel_id=1, replica_groups=mesh['row'=16,'col'=16] {'col'}, use_global_device_ids=true, to_apply=%region_46.47 | all-reduce | flops 8192 | bytes 65536 | tf_op jit(solution)/shard_map/psum | solution.py:82
  845.0 1.7 fusion.97
  850.3 88.5 %all-reduce.15.cloned.1.call-done = (f32[8192]{0:T(1024)}, f32[8192]{0:T(1024)}) async-done(((f32[8192]{0:T(1024)}, f32[8192]{0:T(1024)}), (f32[8192]{0:T(1024)}, f32[8192]{0:T(1024)})) %all-reduce.15.cloned.1.call-update) | async-done | bytes 65552 | tf_op jit(solution)/shard_map/psum | solution.py:88
  941.5 77.5 %all-reduce.3 = (f32[]{:T(128)}, f32[]{:T(128)}, f32[]{:T(128)}, f32[]{:T(128)}, f32[]{:T(128)}) all-reduce(f32[]{:T(128)S(6)} %mul.750, f32[]{:T(128)S(6)} %mul.757, f32[]{:T(128)S(6)} %mul.759, f32[]{:T(128)S(6)} %mul.775, f32[]{:T(128)S(6)} %mul.778), channel_id=1, replica_groups=mesh['row'=16,'col'=16] {'row','col'}, use_global_device_ids=true, to_apply=%region_43.44 | all-reduce | flops 5 | bytes 40 | tf_op jit(solution)/shard_map/psum | solution.py:122
  1022.6 1.7 fusion.99
  1026.0 88.5 %all-reduce.13.cloned.1.call-done = (f32[8192]{0:T(1024)}, f32[8192]{0:T(1024)}) async-done(((f32[8192]{0:T(1024)}, f32[8192]{0:T(1024)}), (f32[8192]{0:T(1024)}, f32[8192]{0:T(1024)})) %all-reduce.13.cloned.1.call-update) | async-done | bytes 65552 | tf_op jit(solution)/shard_map/psum | solution.py:82
  1118.1 43.5 %psum.323 = f32[8192]{0:T(1024)S(1)} all-reduce(f32[8192]{0:T(1024)S(1)} %bitcast.329), channel_id=1, replica_groups=mesh['row'=16,'col'=16] {'row'}, use_global_device_ids=true, to_apply=%region_73.74 | all-reduce | flops 8192 | bytes 65536 | tf_op jit(solution)/shard_map/psum | solution.py:88
  1164.2 77.8 %all-reduce.2 = (f32[]{:T(128)}, f32[]{:T(128)}, f32[]{:T(128)}) all-reduce(f32[]{:T(128)S(6)} %mul.783, f32[]{:T(128)S(6)} %mul.790, f32[]{:T(128)S(6)} %mul.792), channel_id=1, replica_groups=mesh['row'=16,'col'=16] {'row','col'}, use_global_device_ids=true, to_apply=%region_62.63 | all-reduce | flops 3 | bytes 24 | tf_op jit(solution)/shard_map/psum | solution.py:122
  1244.4 1.7 fusion.93
  1247.1 70.4 %psum.326 = f32[8192]{0:T(1024)S(1)} all-reduce(f32[8192]{0:T(1024)S(1)} %bitcast.330), channel_id=1, replica_groups=mesh['row'=16,'col'=16] {'col'}, use_global_device_ids=true, to_apply=%region_80.81 | all-reduce | flops 8192 | bytes 65536 | tf_op jit(solution)/shard_map/psum | solution.py:82
  1320.3 42.5 %psum.328 = f32[8192]{0:T(1024)S(1)} all-reduce(f32[8192]{0:T(1024)S(1)} %bitcast.331), channel_id=1, replica_groups=mesh['row'=16,'col'=16] {'row'}, use_global_device_ids=true, to_apply=%region_85.86 | all-reduce | flops 8192 | bytes 65536 | tf_op jit(solution)/shard_map/psum | solution.py:88
  1365.5 74.6 %all-reduce.1 = (f32[]{:T(128)}, f32[]{:T(128)}, f32[]{:T(128)}) all-reduce(f32[]{:T(128)S(6)} %mul.799, f32[]{:T(128)S(6)} %mul.806, f32[]{:T(128)S(6)} %mul.808), channel_id=1, replica_groups=mesh['row'=16,'col'=16] {'row','col'}, use_global_device_ids=true, to_apply=%region_77.78 | all-reduce | flops 3 | bytes 24 | tf_op jit(solution)/shard_map/psum | solution.py:122
  1445.2 71.0 %psum.331 = f32[8192]{0:T(1024)S(1)} all-reduce(f32[8192]{0:T(1024)S(1)} %bitcast.332), channel_id=1, replica_groups=mesh['row'=16,'col'=16] {'col'}, use_global_device_ids=true, to_apply=%region_92.93 | all-reduce | flops 8192 | bytes 65536 | tf_op jit(solution)/shard_map/psum | solution.py:82
  1518.9 43.1 %psum.333 = f32[8192]{0:T(1024)S(1)} all-reduce(f32[8192]{0:T(1024)S(1)} %bitcast.333), channel_id=1, replica_groups=mesh['row'=16,'col'=16] {'row'}, use_global_device_ids=true, to_apply=%region_97.98 | all-reduce | flops 8192 | bytes 65536 | tf_op jit(solution)/shard_map/psum | solution.py:88
  1564.7 74.6 %all-reduce = (f32[]{:T(128)}, f32[]{:T(128)}, f32[]{:T(128)}) all-reduce(f32[]{:T(128)S(6)} %mul.815, f32[]{:T(128)S(6)} %mul.822, f32[]{:T(128)S(6)} %mul.824), channel_id=1, replica_groups=mesh['row'=16,'col'=16] {'row','col'}, use_global_device_ids=true, to_apply=%region_89.90 | all-reduce | flops 3 | bytes 24 | tf_op jit(solution)/shard_map/psum | solution.py:122
  1642.3 1.7 fusion.85
  1645.0 71.0 %psum.335 = f32[8192]{0:T(1024)S(1)} all-reduce(f32[8192]{0:T(1024)S(1)} %bitcast.317), channel_id=1, replica_groups=mesh['row'=16,'col'=16] {'col'}, use_global_device_ids=true, to_apply=%region_102.103 | all-reduce | flops 8192 | bytes 65536 | tf_op jit(solution)/shard_map/psum | solution.py:82
  (154 shorter events, 65.4 us)
Async XLA Ops:
  7.2 0.8 copy-start.1
  7.2 1.4 copy-start.2
  7.2 161.9 %copy-start = (f32[1,1,16,128,128]{4,3,2,1,0:T(8,128)S(1)}, f32[1,1,16,128,128]{4,3,2,1,0:T(8,128)}, u32[]{:S(2)}) copy-start(f32[1,1,16,128,128]{4,3,2,1,0:T(8,128)} %param.43) | copy-start | bytes 3145732
  7.2 931.6 %all-reduce.15.cloned.1.call-start = ((), (), s32[]{:S(2)}) async-start(), calls=%async_computation.1 | async-start | bytes 131072 | tf_op jit(solution)/shard_map/psum | solution.py:88
  91.7 76.6 %copy-start.3 = (f32[8192]{0:T(1024)S(1)}, f32[8192]{0:T(1024)}, u32[]{:S(2)}) copy-start(f32[8192]{0:T(1024)} %param.48) | copy-start | bytes 98308
  91.7 76.6 %copy-start.11 = (s32[8192]{0:T(1024)S(1)}, s32[8192]{0:T(1024)}, u32[]{:S(2)}) copy-start(s32[8192]{0:T(1024)} %param.49) | copy-start | bytes 98308
  168.3 0.7 copy-start.12
  170.9 0.7 copy-start.13
  172.5 70.9 %copy-start.10 = (s32[8192]{0:T(1024)S(1)}, s32[8192]{0:T(1024)}, u32[]{:S(2)}) copy-start(s32[8192]{0:T(1024)} %param.51) | copy-start | bytes 98308
  841.6 0.6 copy-start.4
  844.1 0.6 copy-start.5
  844.8 269.7 %all-reduce.13.cloned.1.call-start = ((), (), s32[]{:S(2)}) async-start(), calls=%async_computation | async-start | bytes 131072 | tf_op jit(solution)/shard_map/psum | solution.py:82
  847.8 0.6 copy-start.6
  940.2 82.1 %copy-start.8 = (f32[8192]{0:T(1024)S(1)}, f32[8192]{0:T(1024)}, u32[]{:S(2)}) copy-start(f32[8192]{0:T(1024)} %get-tuple-element.1828) | copy-start | bytes 98308
  1025.3 0.6 copy-start.7
  1247.1 70.4 %copy-start.9 = (f32[8192]{0:T(1024)S(1)}, f32[8192]{0:T(1024)}, u32[]{:S(2)}) copy-start(f32[8192]{0:T(1024)} %get-tuple-element.1827) | copy-start | bytes 98308
Sparse Core Ops, SparseCore 0:
  844.9 93.8 all-reduce.14
  1026.1 88.3 all-reduce.12
where the time goes:
time: 1730 us; the launch traced here: 1720 us
  blocking collectives  1430 us (83%)
  waiting for transfers between devices  177 us (10%)
  between operations  49.5 us (3%)
  matrix products  31.9 us (2%)
  other arithmetic  28 us (2%)
    psum x7, blocking collectives, per_device(): lax.psum((jnp.sum(primal_move * (next_col - col_image)) * primal_mask, jn...  528 us
    psum x7, blocking collectives, forward(): return lax.psum(partial_rows, 'col')  496 us
    psum x6, blocking collectives, backward(): return lax.psum(partial_cols, 'row')  256 us
    psum x1, waiting for transfers between devices, backward(): return lax.psum(partial_cols, 'row')  88.5 us
    psum x1, waiting for transfers between devices, forward(): return lax.psum(partial_rows, 'col')  88.5 us
    psum x1, blocking collectives, pair_sums(): lax.psum((primal_term * primal_mask, dual_term * dual_mask), ('row', 'col'))  79.8 us
    pmax x1, blocking collectives, per_device(): largest = lax.pmax(local_largest, ('row', 'col'))  73.6 us
  transfers between devices with their start and end apart: 2, of which 2 were waited for; matrix products, arithmetic and copies ran while one was open for 0% of the time, Pallas kernels for 0%

commit v1 on v0

--- a/solution.py
+++ b/solution.py
@@ -85,7 +85,7 @@
         partial_cols = tile_products(
             tile_data, row_slots, col_slots, live_count, vector, "backward"
         )
-        return lax.psum(partial_cols, "row")
+        return jnp.sum(lax.all_gather(partial_cols, "row"), axis=0)
 
     def pair_sums(primal_term, dual_term):
         return lax.psum((primal_term * primal_mask, dual_term * dual_mask), ("row", "col"))

time: 1730 us -> 1510 us (0.87)
  blocking collectives: 1430 us -> 1300 us
  waiting for transfers between devices: 177 us -> 88 us
    psum x6 -> x0, blocking collectives: 256 us -> none  [backward(): return lax.psum(partial_cols, 'row')]
    all_gather x0 -> x8, blocking collectives: none -> 126 us  [backward(): return jnp.sum(lax.all_gather(partial_cols, 'row'), axis=0)]
    psum x1 -> x0, waiting for transfers between devices: 88.5 us -> none  [backward(): return lax.psum(partial_cols, 'row')]
  transfers between devices with their start and end apart: 2 -> 1, of which waited for: 2 -> 1; matrix products, arithmetic and copies ran while one was open for 0% -> 0% of each run, Pallas kernels for 0% -> 0%
where the time goes in v1:
time: 1510 us
  blocking collectives  1300 us (86%)
  waiting for transfers between devices  88 us (6%)
  between operations  49.4 us (3%)
  matrix products  31.9 us (2%)
  other arithmetic  29.9 us (2%)
    psum x7, blocking collectives, per_device(): lax.psum((jnp.sum(primal_move * (next_col - col_image)) * primal_mask, jn...  529 us
    psum x7, blocking collectives, forward(): return lax.psum(partial_rows, 'col')  495 us
    all_gather x8, blocking collectives, backward(): return jnp.sum(lax.all_gather(partial_cols, 'row'), axis=0)  126 us
    psum x1, waiting for transfers between devices, forward(): return lax.psum(partial_rows, 'col')  88 us
    psum x1, blocking collectives, pair_sums(): lax.psum((primal_term * primal_mask, dual_term * dual_mask), ('row', 'col'))  79.8 us
    pmax x1, blocking collectives, per_device(): largest = lax.pmax(local_largest, ('row', 'col'))  73.6 us
  transfers between devices with their start and end apart: 1, of which 1 were waited for; matrix products, arithmetic and copies ran while one was open for 0% of the time, Pallas kernels for 0%

profile of v1, /device:TPU:32, one launch (start us, length us, event | category | flops | bytes accessed | tf_op | source)
XLA Modules:
  0.0 1505.8 jit_solution(9867328412182189689)
XLA Ops:
  10.5 79.8 %all-reduce.7 = (f32[]{:T(128)}, f32[]{:T(128)}) all-reduce(f32[]{:T(128)S(6)} %mul.700, f32[]{:T(128)S(6)} %mul.702), channel_id=1, replica_groups=mesh['row'=16,'col'=16] {'row','col'}, use_global_device_ids=true, to_apply=%region_1.0 | all-reduce | flops 2 | bytes 16 | tf_op jit(solution)/shard_map/psum | solution.py:91
  91.7 2.2 fusion.120
  93.9 73.6 %pmax.7 = f32[]{:T(128)} all-reduce(f32[]{:T(128)} %fusion.120), channel_id=1, replica_groups=mesh['row'=16,'col'=16] {'row','col'}, use_global_device_ids=true, to_apply=%region_5.0 | all-reduce | flops 1 | bytes 8 | tf_op jit(solution)/shard_map/pmax | solution.py:95
  169.1 1.7 fusion.117
  172.5 70.9 %psum.241 = f32[8192]{0:T(1024)S(1)} all-reduce(f32[8192]{0:T(1024)S(1)} %bitcast.326), channel_id=1, replica_groups=mesh['row'=16,'col'=16] {'col'}, use_global_device_ids=true, to_apply=%region_10.11 | all-reduce | flops 8192 | bytes 65536 | tf_op jit(solution)/shard_map/psum | solution.py:82
  246.2 15.5 %all-gather = f32[16,1,8192]{2,1,0:T(1,128)S(1)} all-gather(f32[1,1,8192]{2,1,0:T(1,128)S(1)} %bitcast.317), channel_id=1, replica_groups=mesh['row'=16,'col'=16] {'row'}, dimensions={0}, use_global_device_ids=true | all-gather | bytes 557056 | tf_op jit(solution)/shard_map/all_gather | solution.py:88
  264.8 75.5 %all-reduce.6 = (f32[]{:T(128)}, f32[]{:T(128)}, f32[]{:T(128)}) all-reduce(f32[]{:T(128)S(6)} %mul.708, f32[]{:T(128)S(6)} %mul.715, f32[]{:T(128)S(6)} %mul.717), channel_id=1, replica_groups=mesh['row'=16,'col'=16] {'row','col'}, use_global_device_ids=true, to_apply=%region_7.8 | all-reduce | flops 3 | bytes 24 | tf_op jit(solution)/shard_map/psum | solution.py:122
  342.5 1.7 fusion.113
  345.2 70.7 %psum.245 = f32[8192]{0:T(1024)S(1)} all-reduce(f32[8192]{0:T(1024)S(1)} %bitcast.327), channel_id=1, replica_groups=mesh['row'=16,'col'=16] {'col'}, use_global_device_ids=true, to_apply=%region_22.23 | all-reduce | flops 8192 | bytes 65536 | tf_op jit(solution)/shard_map/psum | solution.py:82
  418.7 15.5 %all-gather.1 = f32[16,1,8192]{2,1,0:T(1,128)S(1)} all-gather(f32[1,1,8192]{2,1,0:T(1,128)S(1)} %bitcast.318), channel_id=1, replica_groups=mesh['row'=16,'col'=16] {'row'}, dimensions={0}, use_global_device_ids=true | all-gather | bytes 557056 | tf_op jit(solution)/shard_map/all_gather | solution.py:88
  437.2 75.5 %all-reduce.5 = (f32[]{:T(128)}, f32[]{:T(128)}, f32[]{:T(128)}) all-reduce(f32[]{:T(128)S(6)} %mul.722, f32[]{:T(128)S(6)} %mul.729, f32[]{:T(128)S(6)} %mul.731), channel_id=1, replica_groups=mesh['row'=16,'col'=16] {'row','col'}, use_global_device_ids=true, to_apply=%region_19.20 | all-reduce | flops 3 | bytes 24 | tf_op jit(solution)/shard_map/psum | solution.py:122
  517.7 70.8 %psum.249 = f32[8192]{0:T(1024)S(1)} all-reduce(f32[8192]{0:T(1024)S(1)} %bitcast.328), channel_id=1, replica_groups=mesh['row'=16,'col'=16] {'col'}, use_global_device_ids=true, to_apply=%region_34.35 | all-reduce | flops 8192 | bytes 65536 | tf_op jit(solution)/shard_map/psum | solution.py:82
  591.3 15.5 %all-gather.2 = f32[16,1,8192]{2,1,0:T(1,128)S(1)} all-gather(f32[1,1,8192]{2,1,0:T(1,128)S(1)} %bitcast.319), channel_id=1, replica_groups=mesh['row'=16,'col'=16] {'row'}, dimensions={0}, use_global_device_ids=true | all-gather | bytes 557056 | tf_op jit(solution)/shard_map/all_gather | solution.py:88
  609.9 75.5 %all-reduce.4 = (f32[]{:T(128)}, f32[]{:T(128)}, f32[]{:T(128)}) all-reduce(f32[]{:T(128)S(6)} %mul.736, f32[]{:T(128)S(6)} %mul.743, f32[]{:T(128)S(6)} %mul.745), channel_id=1, replica_groups=mesh['row'=16,'col'=16] {'row','col'}, use_global_device_ids=true, to_apply=%region_31.32 | all-reduce | flops 3 | bytes 24 | tf_op jit(solution)/shard_map/psum | solution.py:122
  688.3 1.7 fusion.105
  691.0 70.7 %psum.253 = f32[8192]{0:T(1024)S(1)} all-reduce(f32[8192]{0:T(1024)S(1)} %bitcast.329), channel_id=1, replica_groups=mesh['row'=16,'col'=16] {'col'}, use_global_device_ids=true, to_apply=%region_46.47 | all-reduce | flops 8192 | bytes 65536 | tf_op jit(solution)/shard_map/psum | solution.py:82
  765.1 15.5 %all-gather.3 = f32[16,1,8192]{2,1,0:T(1,128)S(1)} all-gather(f32[1,1,8192]{2,1,0:T(1,128)S(1)} %bitcast.320), channel_id=1, replica_groups=mesh['row'=16,'col'=16] {'row'}, dimensions={0}, use_global_device_ids=true | all-gather | bytes 557056 | tf_op jit(solution)/shard_map/all_gather | solution.py:88
  784.7 75.6 %all-reduce.3 = (f32[]{:T(128)}, f32[]{:T(128)}, f32[]{:T(128)}, f32[]{:T(128)}, f32[]{:T(128)}) all-reduce(f32[]{:T(128)S(6)} %mul.750, f32[]{:T(128)S(6)} %mul.757, f32[]{:T(128)S(6)} %mul.759, f32[]{:T(128)S(6)} %mul.775, f32[]{:T(128)S(6)} %mul.778), channel_id=1, replica_groups=mesh['row'=16,'col'=16] {'row','col'}, use_global_device_ids=true, to_apply=%region_43.44 | all-reduce | flops 5 | bytes 40 | tf_op jit(solution)/shard_map/psum | solution.py:122
  865.9 15.5 %all-gather.4 = f32[16,1,8192]{2,1,0:T(1,128)S(1)} all-gather(f32[1,1,8192]{2,1,0:T(1,128)S(1)} %bitcast.321), channel_id=1, replica_groups=mesh['row'=16,'col'=16] {'row'}, dimensions={0}, use_global_device_ids=true | all-gather | bytes 557056 | tf_op jit(solution)/shard_map/all_gather | solution.py:88
  882.2 1.7 fusion.99
  888.6 88.0 %all-reduce.11.cloned.1.call-done = (f32[8192]{0:T(1024)}, f32[8192]{0:T(1024)}) async-done(((f32[8192]{0:T(1024)}, f32[8192]{0:T(1024)}), (f32[8192]{0:T(1024)}, f32[8192]{0:T(1024)})) %all-reduce.11.cloned.1.call-update) | async-done | bytes 65552 | tf_op jit(solution)/shard_map/psum | solution.py:82
  980.1 17.5 %all-gather.5 = f32[16,1,8192]{2,1,0:T(1,128)S(1)} all-gather(f32[1,1,8192]{2,1,0:T(1,128)S(1)} %bitcast.322), channel_id=1, replica_groups=mesh['row'=16,'col'=16] {'row'}, dimensions={0}, use_global_device_ids=true | all-gather | bytes 557056 | tf_op jit(solution)/shard_map/all_gather | solution.py:88
  1000.5 75.8 %all-reduce.2 = (f32[]{:T(128)}, f32[]{:T(128)}, f32[]{:T(128)}) all-reduce(f32[]{:T(128)S(6)} %mul.783, f32[]{:T(128)S(6)} %mul.790, f32[]{:T(128)S(6)} %mul.792), channel_id=1, replica_groups=mesh['row'=16,'col'=16] {'row','col'}, use_global_device_ids=true, to_apply=%region_62.63 | all-reduce | flops 3 | bytes 24 | tf_op jit(solution)/shard_map/psum | solution.py:122
  1081.4 70.9 %psum.264 = f32[8192]{0:T(1024)S(1)} all-reduce(f32[8192]{0:T(1024)S(1)} %bitcast.332), channel_id=1, replica_groups=mesh['row'=16,'col'=16] {'col'}, use_global_device_ids=true, to_apply=%region_80.81 | all-reduce | flops 8192 | bytes 65536 | tf_op jit(solution)/shard_map/psum | solution.py:82
  1155.0 15.5 %all-gather.6 = f32[16,1,8192]{2,1,0:T(1,128)S(1)} all-gather(f32[1,1,8192]{2,1,0:T(1,128)S(1)} %bitcast.323), channel_id=1, replica_groups=mesh['row'=16,'col'=16] {'row'}, dimensions={0}, use_global_device_ids=true | all-gather | bytes 557056 | tf_op jit(solution)/shard_map/all_gather | solution.py:88
  1173.6 75.5 %all-reduce.1 = (f32[]{:T(128)}, f32[]{:T(128)}, f32[]{:T(128)}) all-reduce(f32[]{:T(128)S(6)} %mul.799, f32[]{:T(128)S(6)} %mul.806, f32[]{:T(128)S(6)} %mul.808), channel_id=1, replica_groups=mesh['row'=16,'col'=16] {'row','col'}, use_global_device_ids=true, to_apply=%region_77.78 | all-reduce | flops 3 | bytes 24 | tf_op jit(solution)/shard_map/psum | solution.py:122
  1251.4 1.7 fusion.89
  1254.2 70.7 %psum.268 = f32[8192]{0:T(1024)S(1)} all-reduce(f32[8192]{0:T(1024)S(1)} %bitcast.333), channel_id=1, replica_groups=mesh['row'=16,'col'=16] {'col'}, use_global_device_ids=true, to_apply=%region_92.93 | all-reduce | flops 8192 | bytes 65536 | tf_op jit(solution)/shard_map/psum | solution.py:82
  1327.6 15.5 %all-gather.7 = f32[16,1,8192]{2,1,0:T(1,128)S(1)} all-gather(f32[1,1,8192]{2,1,0:T(1,128)S(1)} %bitcast.324), channel_id=1, replica_groups=mesh['row'=16,'col'=16] {'row'}, dimensions={0}, use_global_device_ids=true | all-gather | bytes 557056 | tf_op jit(solution)/shard_map/all_gather | solution.py:88
  1346.2 75.8 %all-reduce = (f32[]{:T(128)}, f32[]{:T(128)}, f32[]{:T(128)}) all-reduce(f32[]{:T(128)S(6)} %mul.815, f32[]{:T(128)S(6)} %mul.822, f32[]{:T(128)S(6)} %mul.824), channel_id=1, replica_groups=mesh['row'=16,'col'=16] {'row','col'}, use_global_device_ids=true, to_apply=%region_89.90 | all-reduce | flops 3 | bytes 24 | tf_op jit(solution)/shard_map/psum | solution.py:122
  1424.9 1.7 fusion.85
  1427.7 70.7 %psum.271 = f32[8192]{0:T(1024)S(1)} all-reduce(f32[8192]{0:T(1024)S(1)} %bitcast.325), channel_id=1, replica_groups=mesh['row'=16,'col'=16] {'col'}, use_global_device_ids=true, to_apply=%region_102.103 | all-reduce | flops 8192 | bytes 65536 | tf_op jit(solution)/shard_map/psum | solution.py:82
  (155 shorter events, 68.2 us)
Async XLA Ops:
  7.2 0.8 copy-start.1
  7.2 1.4 copy-start.2
  7.2 161.9 %copy-start = (f32[1,1,16,128,128]{4,3,2,1,0:T(8,128)S(1)}, f32[1,1,16,128,128]{4,3,2,1,0:T(8,128)}, u32[]{:S(2)}) copy-start(f32[1,1,16,128,128]{4,3,2,1,0:T(8,128)} %param.43) | copy-start | bytes 3145732
  7.2 969.4 %all-reduce.11.cloned.1.call-start = ((), (), s32[]{:S(2)}) async-start(), calls=%async_computation | async-start | bytes 131072 | tf_op jit(solution)/shard_map/psum | solution.py:82
  91.7 76.6 %copy-start.3 = (f32[8192]{0:T(1024)S(1)}, f32[8192]{0:T(1024)}, u32[]{:S(2)}) copy-start(f32[8192]{0:T(1024)} %param.48) | copy-start | bytes 98308
  91.7 76.6 %copy-start.8 = (s32[8192]{0:T(1024)S(1)}, s32[8192]{0:T(1024)}, u32[]{:S(2)}) copy-start(s32[8192]{0:T(1024)} %param.49) | copy-start | bytes 98308
  168.3 0.7 copy-start.9
  170.9 0.7 copy-start.10
  172.5 70.9 %copy-start.7 = (s32[8192]{0:T(1024)S(1)}, s32[8192]{0:T(1024)}, u32[]{:S(2)}) copy-start(s32[8192]{0:T(1024)} %param.51) | copy-start | bytes 98308
  884.9 1.7 copy-start.4
  887.9 0.6 copy-start.5
  1081.3 70.9 %copy-start.6 = (f32[8192]{0:T(1024)S(1)}, f32[8192]{0:T(1024)}, u32[]{:S(2)}) copy-start(f32[8192]{0:T(1024)} %get-tuple-element.1827) | copy-start | bytes 98308
Sparse Core Ops, SparseCore 0:
  888.7 87.8 all-reduce.10
